TPU v7x, 32 devices: a whole 2x2x4 slice. The times are simulated.
32 devices in a mesh: dp: 8 (over z, x), tensor: 4 (over y, core).
Axes of the slice: x: 2, y: 2, z: 4, core: 2. Of those that a mesh axis runs over, the one named last changes fastest.
Arguments:
- context: bfloat16 [2, 8192, 3072], P(None, 'dp', 'tensor'), may hold values from -6 to 6
- out_grad: bfloat16 [2, 8192, 3072], P(None, ('dp', 'tensor')), may hold values from -0.1875 to 0.1875
- error_in: bfloat16 [2, 24576, 3072], P(None, 'dp', 'tensor'), may hold values from -6 to 6
- right_init: float32 [2, 64, 3072], P(None, None, 'tensor'), may hold values from -6 to 6
Outputs:
- summed_update: bfloat16 [2, 3072, 3072], P(None, 'dp', 'tensor')
- error_out: bfloat16 [2, 24576, 3072], P(None, 'dp', 'tensor')
All inputs are finite; a program needn't handle non-finite values.
Results may differ from a plain program's by a relative error of at most 0.015.
Values may be sent and summed in bfloat16 or wider, within the bound.
A program may use at most 128 MiB of HBM per device.

v0:
```python
import jax
import jax.numpy as jnp
from jax import lax
from jax.sharding import PartitionSpec as P


def solve_rows(gram_matrix, left_factor):
    ridge_term = 1e-06 * jnp.mean(jnp.diagonal(gram_matrix, axis1=1, axis2=2), axis=1)
    eye_matrix = jnp.eye(gram_matrix.shape[1], dtype=gram_matrix.dtype)
    gram_matrix = gram_matrix + ridge_term[:, None, None] * eye_matrix
    factor_low = jnp.linalg.cholesky(gram_matrix)

    def one_solve(low_part, rhs_part):
        return jax.scipy.linalg.solve_triangular(low_part, rhs_part, lower=True)

    return jax.vmap(one_solve)(factor_low, left_factor)


def gram_of(left_factor):
    return jnp.einsum("lrd,lsd->lrs", left_factor, left_factor, precision=lax.Precision.HIGHEST)


def compress(context, out_grad, error_in, right_init):
    out_width = out_grad.shape[2]
    moment = jnp.einsum(
        "ltd,lte->lde",
        lax.all_gather(out_grad, "tensor", axis=1, tiled=True),
        context,
        preferred_element_type=jnp.float32,
    )
    moment = moment + error_in.astype(jnp.float32)
    left_factor = jnp.einsum("lre,lde->lrd", right_init, moment, precision=lax.Precision.HIGHEST)
    left_part = lax.psum_scatter(left_factor, "tensor", scatter_dimension=2, tiled=True)
    left_part = lax.psum(left_part, "dp")
    gram_matrix = lax.psum(gram_of(left_part), "tensor")
    ortho_part = solve_rows(gram_matrix, left_part)
    ortho_basis = lax.all_gather(ortho_part, "tensor", axis=2, tiled=True)
    right_terms = jnp.einsum("lrd,lde->lre", ortho_basis, moment, precision=lax.Precision.HIGHEST)
    right_factor = lax.psum(right_terms.astype(jnp.bfloat16), "dp").astype(jnp.float32)
    replicas = lax.axis_size("dp")
    row_share = out_width // replicas
    own_basis = lax.dynamic_slice_in_dim(
        ortho_basis, lax.axis_index("dp") * row_share, row_share, 2
    )
    summed = jnp.einsum("lrd,lre->lde", own_basis, right_factor, precision=lax.Precision.HIGHEST)
    mean_part = jnp.einsum(
        "lrd,lre->lde", ortho_basis, right_factor / replicas, precision=lax.Precision.HIGHEST
    )
    new_error = (moment - mean_part).astype(jnp.bfloat16)
    return (summed.astype(jnp.bfloat16), new_error)


def body(context, out_grad, error_in, right_init):
    return compress(context, out_grad, error_in, right_init)


def solution(mesh):
    return jax.shard_map(
        body,
        mesh=mesh,
        in_specs=(
            P(None, "dp", "tensor"),
            P(None, ("dp", "tensor"), None),
            P(None, "dp", "tensor"),
            P(None, None, "tensor"),
        ),
        out_specs=(P(None, "dp", "tensor"), P(None, "dp", "tensor")),
        check_vma=False,
    )
```

profile of v0, /device:TPU:0, one launch (start us, length us, event | category | flops | bytes accessed | tf_op | source)
XLA Modules:
  0.0 419.1 jit_solution(9212171889300298580)
XLA Ops:
  7.2 0.0 all-gather.3.cloned.1.call-start
  7.2 4.8 %copy.12 = bf16[2,256,3072]{1,2,0:T(8,128)(2,1)} copy(bf16[2,256,3072]{2,1,0:T(8,128)(2,1)} %param.5) | data formatting | bytes 6291456 | tf_op args[1]
  12.0 0.0 all-gather.3.cloned.1.call-update
  12.0 0.0 reduce-scatter.2.cloned.1.call-start
  12.1 86.6 %all-gather.3.cloned.1.call-done = bf16[2,1024,3072]{1,2,0:T(8,128)(2,1)} async-done(((bf16[2,256,3072]{1,2,0:T(8,128)(2,1)}), bf16[2,1024,3072]{1,2,0:T(8,128)(2,1)}) %all-gather.3.cloned.1.call-update) | async-done | bytes 12582928 | tf_op jit(solution)/shard_map/all_gather | solution.py:27
  98.7 19.3 %convert_add_fusion = f32[2,3072,768]{2,1,0:T(8,128)} fusion(bf16[2,3072,768]{2,1,0:T(8,128)(2,1)} %param.6, bf16[2,1024,3072]{1,2,0:T(8,128)(2,1)} %all-gather.3.cloned.1.call-done, bf16[2,1024,768]{2,1,0:T(8,128)(2,1)S(1)} %copy-done), kind=kOutput, calls=%fused_computation.2 | convolution fusion | flops 9673113600 | bytes 44040192 | tf_op jit(solution)/shard_map/ltd,lte->lde/dot_general | solution.py:25
  118.0 22.5 %convolution_bitcast_fusion = f32[2,64,3072]{2,1,0:T(8,128)} fusion(f32[2,3072,768]{2,1,0:T(8,128)} %convert_add_fusion, f32[2,64,768]{2,1,0:T(8,128)S(1)} %copy-done.4), kind=kOutput, calls=%fused_computation.3 | convolution fusion | flops 3623878656 | bytes 20840448 | tf_op jit(solution)/shard_map/lre,lde->lrd/dot_general | solution.py:32
  140.5 0.0 all-reduce.3.cloned.1.call-start
  140.5 28.1 %reduce-scatter.2.cloned.1.call-done = f32[2,64,768]{2,1,0:T(8,128)} async-done(((f32[2,64,3072]{2,1,0:T(8,128)}), f32[2,64,768]{2,1,0:T(8,128)}) %reduce-scatter.2.cloned.1.call-update) | async-done | bytes 393232 | tf_op jit(solution)/shard_map/reduce_scatter | solution.py:33
  168.6 0.0 all-reduce.3.cloned.1.call-update
  168.7 0.0 all-gather.5.cloned.1.call-start
  168.7 0.1 copy.15
  168.9 75.0 %all-reduce.3.cloned.1.call-done = f32[2,64,768]{2,1,0:T(8,128)} async-done(((f32[2,64,768]{2,1,0:T(8,128)}), f32[2,64,768]{2,1,0:T(8,128)}) %all-reduce.3.cloned.1.call-update) | async-done | bytes 393232 | tf_op jit(solution)/shard_map/psum | solution.py:34
  243.9 1.7 fusion.10
  245.5 10.9 %psum.22 = f32[2,64,64]{1,2,0:T(8,128)S(1)} all-reduce(f32[2,64,64]{1,2,0:T(8,128)S(1)} %fusion.10), channel_id=1, replica_groups=mesh['dp'=8,'tensor'=4] {'tensor'}, use_global_device_ids=true, to_apply=%region_2.0 | all-reduce | flops 8192 | bytes 65536 | tf_op jit(solution)/shard_map/psum | solution.py:35
  256.4 1.9 copy.14
  258.3 0.9 gather_fusion
  259.3 0.1 multiply_add_fusion
  259.3 0.1 copy.16
  259.4 0.1 fusion.6
  259.5 11.7 %custom-call.8 = f32[2,64,64]{2,1,0:T(8,128)S(1)} custom-call(f32[2,64,64]{2,1,0:T(8,128)S(1)} %fusion.6), custom_call_target="Cholesky" | custom-call | tf_op jit(solution)/shard_map/jit(cholesky)/cholesky | solution.py:11
  271.3 0.1 compare_reduce_fusion
  271.4 0.1 select_bitcast_fusion
  271.5 9.8 %custom-call.9 = f32[2,1,64,64]{2,3,1,0:T(8,128)S(1)} custom-call(f32[2,1,64,64]{3,2,1,0:T(8,128)S(1)} %select_bitcast_fusion), custom_call_target="InvertDiagBlocksLowerTriangular" | custom-call | tf_op jit(solution)/shard_map/vmap(jit(_solve_triangular))/triangular_solve | solution.py:14
  281.3 1.3 fusion.4
  282.6 0.0 all-gather.5.cloned.1.call-update
  282.6 0.0 all-reduce.5.cloned.1.call-start
  282.7 18.8 %all-gather.5.cloned.1.call-done = f32[2,64,3072]{2,1,0:T(8,128)} async-done(((f32[2,64,768]{2,1,0:T(8,128)}), f32[2,64,3072]{2,1,0:T(8,128)}) %all-gather.5.cloned.1.call-update) | async-done | bytes 1572880 | tf_op jit(solution)/shard_map/all_gather | solution.py:37
  301.5 16.3 %convolution_convert_fusion.1 = bf16[2,64,768]{2,1,0:T(8,128)(2,1)} fusion(f32[2,64,3072]{2,1,0:T(8,128)} %all-gather.5.cloned.1.call-done, f32[2,3072,768]{2,1,0:T(8,128)} %convert_add_fusion), kind=kOutput, calls=%fused_computation.5 | convolution fusion | flops 3623976960 | bytes 20643840 | tf_op jit(solution)/shard_map/lrd,lde->lre/dot_general | solution.py:38
  317.8 70.8 %all-reduce.5.cloned.1.call-done = bf16[2,64,768]{2,1,0:T(8,128)(2,1)} async-done(((bf16[2,64,768]{2,1,0:T(8,128)(2,1)}), bf16[2,64,768]{2,1,0:T(8,128)(2,1)}) %all-reduce.5.cloned.1.call-update) | async-done | bytes 196624 | tf_op jit(solution)/shard_map/psum | solution.py:39
  388.6 20.9 %subtract_convert_fusion = bf16[2,3072,768]{2,1,0:T(8,128)(2,1)} fusion(f32[2,3072,768]{2,1,0:T(8,128)} %convert_add_fusion, f32[2,64,3072]{2,1,0:T(8,128)} %all-gather.5.cloned.1.call-done, bf16[2,64,768]{2,1,0:T(8,128)(2,1)} %all-reduce.5.cloned.1.call-done), kind=kOutput, calls=%fused_computation.1 | convolution fusion | flops 3633512448 | bytes 30081024 | tf_op jit(solution)/shard_map/lrd,lre->lde/dot_general | solution.py:46
  409.5 3.1 convolution_convert_fusion
  (19 shorter events, 0.2 us)
Async XLA Ops:
  7.2 91.5 %copy-start = (bf16[2,1024,768]{2,1,0:T(8,128)(2,1)S(1)}, bf16[2,1024,768]{2,1,0:T(8,128)(2,1)}, u32[]{:S(2)}) copy-start(bf16[2,1024,768]{2,1,0:T(8,128)(2,1)} %param.4) | copy-start | bytes 9437188
  7.2 91.5 %all-gather.3.cloned.1.call-start = ((), (), s32[]{:S(2)}) async-start(), calls=%async_computation.1 | async-start | bytes 15728640 | tf_op jit(solution)/shard_map/all_gather | solution.py:27
  12.0 105.9 %copy-start.4 = (f32[2,64,768]{2,1,0:T(8,128)S(1)}, f32[2,64,768]{2,1,0:T(8,128)}, u32[]{:S(2)}) copy-start(f32[2,64,768]{2,1,0:T(8,128)} %param.7) | copy-start | bytes 1179652
  12.0 156.6 %reduce-scatter.2.cloned.1.call-start = ((), (), s32[]{:S(2)}) async-start(), calls=%async_computation.2 | async-start | bytes 1966080 | tf_op jit(solution)/shard_map/reduce_scatter | solution.py:33
  140.5 103.4 %all-reduce.3.cloned.1.call-start = ((), (), s32[]{:S(2)}) async-start(), calls=%async_computation.3 | async-start | bytes 786432 | tf_op jit(solution)/shard_map/psum | solution.py:34
  168.7 132.8 %all-gather.5.cloned.1.call-start = ((), (), s32[]{:S(2)}) async-start(), calls=%async_computation.4 | async-start | bytes 1966080 | tf_op jit(solution)/shard_map/all_gather | solution.py:37
  243.9 37.5 %copy-start.2 = (f32[2,64,768]{2,1,0:T(8,128)S(1)}, f32[2,64,768]{2,1,0:T(8,128)}, u32[]{:S(2)}) copy-start(f32[2,64,768]{2,1,0:T(8,128)} %all-reduce.3.cloned.1.call-done) | copy-start | bytes 1179652
  282.6 106.0 %all-reduce.5.cloned.1.call-start = ((), (), s32[]{:S(2)}) async-start(), calls=%async_computation.5 | async-start | bytes 393216 | tf_op jit(solution)/shard_map/psum | solution.py:39
  388.6 20.9 %copy-start.3 = (bf16[2,64,768]{2,1,0:T(8,128)(2,1)S(1)}, bf16[2,64,768]{2,1,0:T(8,128)(2,1)}, u32[]{:S(2)}) copy-start(bf16[2,64,768]{2,1,0:T(8,128)(2,1)} %all-reduce.5.cloned.1.call-done) | copy-start | bytes 589828
  388.6 24.0 %copy-start.1 = (bf16[2,1024,768]{2,1,0:T(8,128)(2,1)S(1)}, bf16[2,1024,768]{2,1,0:T(8,128)(2,1)}, u32[]{:S(2)}) copy-start(bf16[2,1024,768]{2,1,0:T(8,128)(2,1)} %param.4) | copy-start | bytes 9437188
Sparse Core Ops, SparseCore 0:
  12.2 86.4 all-gather.2
  140.6 27.9 reduce-scatter.1
  172.0 71.8 all-reduce.2
  282.8 18.6 all-gather.4
  317.9 70.6 all-reduce.4
where the time goes:
time: 419 us
  waiting for transfers between devices  279 us (67%)
  matrix products  85 us (20%)
  other arithmetic  22 us (5%)
  between operations  13.9 us (3%)
  blocking collectives  10.9 us (3%)
  local copies, waits for them, and re-layouts  7.81 us (2%)
    all_gather x1, waiting for transfers between devices, compress(): lax.all_gather(out_grad, 'tensor', axis=1, tiled=True)  86.6 us
    psum x1, waiting for transfers between devices, compress(): left_part = lax.psum(left_part, 'dp')  75 us
    psum x1, waiting for transfers between devices, compress(): lax.psum(right_terms.astype(jnp.bfloat16), 'dp').astype(jnp.float32)  70.8 us
    reduce_scatter x1, waiting for transfers between devices, compress(): lax.psum_scatter(left_factor, 'tensor', scatter_dimension=2, tiled=True)  28.1 us
    dot_general x1, matrix products, compress(): jnp.einsum('lre,lde->lrd', right_init, moment, precision=lax.Precision.HI...  22.5 us
    dot_general x1, matrix products, compress(): jnp.einsum('lrd,lre->lde', ortho_basis, right_factor / replicas, precisio...  20.9 us
    dot_general x1, matrix products, compress(): jnp.einsum('ltd,lte->lde', lax.all_gather(out_grad, 'tensor', axis=1, til...  19.3 us
    all_gather x1, waiting for transfers between devices, compress(): ortho_basis = lax.all_gather(ortho_part, 'tensor', axis=2, tiled=True)  18.8 us
  transfers between devices with their start and end apart: 5, of which 5 were waited for; matrix products, arithmetic and copies ran while one was open for 0% of the time, Pallas kernels for 0%

commit v1 on v0

--- a/solution.py
+++ b/solution.py
@@ -22,12 +22,26 @@
 
 def compress(context, out_grad, error_in, right_init):
     out_width = out_grad.shape[2]
+    length, index = (lax.axis_size("tensor"), lax.axis_index("tensor"))
+    backward = [(i, (i - 1) % length) for i in range(length)]
+    width = out_grad.shape[1]
+    held = out_grad
     moment = jnp.einsum(
         "ltd,lte->lde",
-        lax.all_gather(out_grad, "tensor", axis=1, tiled=True),
-        context,
+        held,
+        lax.dynamic_slice_in_dim(context, index * width, held.shape[1], axis=1),
         preferred_element_type=jnp.float32,
     )
+    for step in range(1, length):
+        held = lax.ppermute(held, "tensor", backward)
+        moment = moment + jnp.einsum(
+            "ltd,lte->lde",
+            held,
+            lax.dynamic_slice_in_dim(
+                context, (index + step) % length * width, held.shape[1], axis=1
+            ),
+            preferred_element_type=jnp.float32,
+        )
     moment = moment + error_in.astype(jnp.float32)
     left_factor = jnp.einsum("lre,lde->lrd", right_init, moment, precision=lax.Precision.HIGHEST)
     left_part = lax.psum_scatter(left_factor, "tensor", scatter_dimension=2, tiled=True)

time: 419 us -> 470 us (1.12)
  matrix products: 85 us -> 123 us
  local copies, waits for them, and re-layouts: 7.81 us -> 30.1 us
  waiting for transfers between devices: 279 us -> 263 us
  starting transfers between devices: 0.2 us -> 6.46 us
    all_gather x1 -> x0, waiting for transfers between devices: 86.6 us -> none  [compress(): lax.all_gather(out_grad, 'tensor', axis=1, tiled=True)]
    ppermute x0 -> x3, waiting for transfers between devices: none -> 69.9 us  [compress(): held = lax.ppermute(held, 'tensor', backward)]
    dot_general x1 -> x4, matrix products: 19.3 us -> 57.4 us  [the longest x3 47.5 us: compress(): jnp.einsum('ltd,lte->lde', held, lax.dynamic_slice_in_dim(context, (index...]
    unnamed x11 -> x18, local copies, waits for them, and re-layouts: 4.83 us -> 27.1 us
    dot_general x1, matrix products: 16.3 us -> 22.8 us  [compress(): jnp.einsum('lrd,lde->lre', ortho_basis, moment, precision=lax.Precision.H...]
    ppermute x0 -> x3, starting transfers between devices: none -> 6.3 us  [compress(): held = lax.ppermute(held, 'tensor', backward)]
    dot_general x1, matrix products: 22.5 us -> 16.5 us  [compress(): jnp.einsum('lre,lde->lrd', right_init, moment, precision=lax.Precision.HI...]
  transfers between devices with their start and end apart: 5 -> 7, of which waited for: 5 -> 6; matrix products, arithmetic and copies ran while one was open for 0% -> 9% of each run, Pallas kernels for 0% -> 0%
where the time goes in v1:
time: 470 us; the launch traced here: 469 us
  waiting for transfers between devices  263 us (56%)
  matrix products  123 us (26%)
  local copies, waits for them, and re-layouts  30.1 us (6%)
  other arithmetic  22 us (5%)
  between operations  13.9 us (3%)
  blocking collectives  10.9 us (2%)
  starting transfers between devices  6.46 us (1%)
    psum x1, waiting for transfers between devices, compress(): left_part = lax.psum(left_part, 'dp')  74.9 us
    psum x1, waiting for transfers between devices, compress(): lax.psum(right_terms.astype(jnp.bfloat16), 'dp').astype(jnp.float32)  70.8 us
    ppermute x3, waiting for transfers between devices, compress(): held = lax.ppermute(held, 'tensor', backward)  69.9 us
    dot_general x3, matrix products, compress(): jnp.einsum('ltd,lte->lde', held, lax.dynamic_slice_in_dim(context, (index...  47.5 us
    reduce_scatter x1, waiting for transfers between devices, compress(): lax.psum_scatter(left_factor, 'tensor', scatter_dimension=2, tiled=True)  28.5 us
    unnamed x18, local copies, waits for them, and re-layouts  27.1 us
    dot_general x1, matrix products, compress(): jnp.einsum('lrd,lde->lre', ortho_basis, moment, precision=lax.Precision.H...  22.8 us
    dot_general x1, matrix products, compress(): jnp.einsum('lrd,lre->lde', ortho_basis, right_factor / replicas, precisio...  19.9 us
  transfers between devices with their start and end apart: 7, of which 6 were waited for; matrix products, arithmetic and copies ran while one was open for 9% of the time, Pallas kernels for 0%

profile of v1, /device:TPU:0, one launch (start us, length us, event | category | flops | bytes accessed | tf_op | source)
XLA Modules:
  0.0 468.8 jit_solution(5994183438253462326)
XLA Ops:
  7.2 2.5 collective-permute-start
  9.7 35.1 %collective-permute-done = bf16[2,256,3072]{2,1,0:T(8,128)(2,1)S(1)} collective-permute-done((bf16[2,256,3072]{2,1,0:T(8,128)(2,1)}, bf16[2,256,3072]{2,1,0:T(8,128)(2,1)S(1)}, u32[]{:S(2)}, u32[]{:S(2)}) %collective-permute-start) | collective-permute-done | bytes 3145760 | tf_op jit(solution)/shard_map/ppermute | solution.py:36
  44.8 1.7 copy-done.4
  46.5 1.8 collective-permute-start.1
  48.3 34.8 %collective-permute-done.1 = bf16[2,256,3072]{2,1,0:T(8,128)(2,1)} collective-permute-done((bf16[2,256,3072]{2,1,0:T(8,128)(2,1)S(1)}, bf16[2,256,3072]{2,1,0:T(8,128)(2,1)}, u32[]{:S(2)}, u32[]{:S(2)}) %collective-permute-start.1) | collective-permute-done | bytes 3145760 | tf_op jit(solution)/shard_map/ppermute | solution.py:36
  83.1 2.0 collective-permute-start.2
  85.1 12.6 %copy.24 = bf16[2,3072,768]{1,2,0:T(8,128)(2,1)} copy(bf16[2,3072,768]{2,1,0:T(8,128)(2,1)} %param.6) | data formatting | bytes 18874368 | tf_op args[2]
  97.7 9.8 %fusion.5 = f32[2,768,3072]{2,1,0:T(8,128)} fusion(bf16[2,256,3072]{2,1,0:T(8,128)(2,1)} %param.5, bf16[2,1024,768]{2,1,0:T(8,128)(2,1)S(1)} %copy-done, s32[]{:T(128)S(6)} %select_n.38), kind=kOutput, calls=%fused_computation.11 | convolution fusion | flops 2415919104 | bytes 22806532 | tf_op jit(solution)/shard_map/ltd,lte->lde/dot_general | solution.py:29
  107.5 7.9 %fusion.3 = f32[2,768,3072]{2,1,0:T(8,128)} fusion(bf16[2,256,3072]{2,1,0:T(8,128)(2,1)S(1)} %copy-done.5, bf16[2,1024,768]{2,1,0:T(8,128)(2,1)S(1)} %copy-done, s32[]{:T(128)S(6)} %select_n.40), kind=kOutput, calls=%fused_computation.9 | convolution fusion | flops 2415919104 | bytes 22806532 | tf_op jit(solution)/shard_map/ltd,lte->lde/dot_general | solution.py:37
  115.5 9.6 %fusion.1 = f32[2,768,3072]{2,1,0:T(8,128)} fusion(bf16[2,256,3072]{2,1,0:T(8,128)(2,1)} %collective-permute-done.1, bf16[2,1024,768]{2,1,0:T(8,128)(2,1)S(1)} %copy-done, s32[]{:T(128)S(6)} %select_n.42), kind=kOutput, calls=%fused_computation.7 | convolution fusion | flops 2415919104 | bytes 22806532 | tf_op jit(solution)/shard_map/ltd,lte->lde/dot_general | solution.py:37
  125.1 30.0 %bitcast_add_fusion = f32[2,3072,768]{1,2,0:T(8,128)} fusion(bf16[2,3072,768]{1,2,0:T(8,128)(2,1)} %copy.24, f32[2,768,3072]{2,1,0:T(8,128)} %fusion.1, f32[2,768,3072]{2,1,0:T(8,128)} %fusion.5, f32[2,768,3072]{2,1,0:T(8,128)} %fusion.3, bf16[2,256,3072]{2,1,0:T(8,128)(2,1)} %collective-permute-done.2, bf16[2,1024,768]{2,1,0:T(8,128)(2,1)S(1)} %copy-done, ...), kind=kOutput, calls=%fused_computation.1 | convolution fusion | flops 2439512064 | bytes 88866816 | tf_op jit(solution)/shard_map/ltd,lte->lde/dot_general | solution.py:37
  155.1 16.5 %convolution_bitcast_fusion = f32[2,64,3072]{2,1,0:T(8,128)} fusion(f32[2,3072,768]{1,2,0:T(8,128)} %bitcast_add_fusion, f32[2,64,768]{2,1,0:T(8,128)S(1)} %copy-done.7), kind=kOutput, calls=%fused_computation.3 | convolution fusion | flops 3623878656 | bytes 20840448 | tf_op jit(solution)/shard_map/lre,lde->lrd/dot_general | solution.py:46
  171.7 28.5 %reduce-scatter.2.cloned.1.call-done = f32[2,64,768]{2,1,0:T(8,128)} async-done(((f32[2,64,3072]{2,1,0:T(8,128)}), f32[2,64,768]{2,1,0:T(8,128)}) %reduce-scatter.2.cloned.1.call-update) | async-done | bytes 393232 | tf_op jit(solution)/shard_map/reduce_scatter | solution.py:47
  200.3 74.9 %all-reduce.3.cloned.1.call-done = f32[2,64,768]{2,1,0:T(8,128)} async-done(((f32[2,64,768]{2,1,0:T(8,128)}), f32[2,64,768]{2,1,0:T(8,128)}) %all-reduce.3.cloned.1.call-update) | async-done | bytes 393232 | tf_op jit(solution)/shard_map/psum | solution.py:48
  275.3 1.7 fusion.21
  276.9 10.9 %psum.22 = f32[2,64,64]{1,2,0:T(8,128)S(1)} all-reduce(f32[2,64,64]{1,2,0:T(8,128)S(1)} %fusion.21), channel_id=1, replica_groups=mesh['dp'=8,'tensor'=4] {'tensor'}, use_global_device_ids=true, to_apply=%region_2.3 | all-reduce | flops 8192 | bytes 65536 | tf_op jit(solution)/shard_map/psum | solution.py:49
  287.8 1.9 copy.27
  289.8 0.9 gather_fusion
  290.7 0.1 multiply_add_fusion
  290.8 0.1 copy.29
  290.9 0.1 fusion.13
  290.9 11.7 %custom-call.8 = f32[2,64,64]{2,1,0:T(8,128)S(1)} custom-call(f32[2,64,64]{2,1,0:T(8,128)S(1)} %fusion.13), custom_call_target="Cholesky" | custom-call | tf_op jit(solution)/shard_map/jit(cholesky)/cholesky | solution.py:11
  302.7 0.1 compare_reduce_fusion
  302.8 0.1 select_bitcast_fusion
  302.9 9.8 %custom-call.9 = f32[2,1,64,64]{2,3,1,0:T(8,128)S(1)} custom-call(f32[2,1,64,64]{3,2,1,0:T(8,128)S(1)} %select_bitcast_fusion), custom_call_target="InvertDiagBlocksLowerTriangular" | custom-call | tf_op jit(solution)/shard_map/vmap(jit(_solve_triangular))/triangular_solve | solution.py:14
  312.8 1.3 fusion.11
  314.1 18.8 %all-gather.2.cloned.1.call-done = f32[2,64,3072]{2,1,0:T(8,128)} async-done(((f32[2,64,768]{2,1,0:T(8,128)}), f32[2,64,3072]{2,1,0:T(8,128)}) %all-gather.2.cloned.1.call-update) | async-done | bytes 1572880 | tf_op jit(solution)/shard_map/all_gather | solution.py:51
  332.9 22.8 %convolution_convert_fusion.1 = bf16[2,64,768]{2,1,0:T(8,128)(2,1)} fusion(f32[2,64,3072]{2,1,0:T(8,128)} %all-gather.2.cloned.1.call-done, f32[2,3072,768]{1,2,0:T(8,128)} %bitcast_add_fusion), kind=kOutput, calls=%fused_computation.5 | convolution fusion | flops 3623976960 | bytes 20643840 | tf_op jit(solution)/shard_map/lrd,lde->lre/dot_general | solution.py:52
  355.7 70.8 %all-reduce.5.cloned.1.call-done = bf16[2,64,768]{2,1,0:T(8,128)(2,1)} async-done(((bf16[2,64,768]{2,1,0:T(8,128)(2,1)}), bf16[2,64,768]{2,1,0:T(8,128)(2,1)}) %all-reduce.5.cloned.1.call-update) | async-done | bytes 196624 | tf_op jit(solution)/shard_map/psum | solution.py:53
  426.5 19.9 %subtract_convert_fusion = bf16[2,3072,768]{1,2,0:T(8,128)(2,1)} fusion(f32[2,3072,768]{1,2,0:T(8,128)} %bitcast_add_fusion, f32[2,64,3072]{2,1,0:T(8,128)S(1)} %copy-done.2, bf16[2,64,768]{2,1,0:T(8,128)(2,1)} %all-reduce.5.cloned.1.call-done), kind=kOutput, calls=%fused_computation.2 | convolution fusion | flops 3633512448 | bytes 30081024 | tf_op jit(solution)/shard_map/lrd,lre->lde/dot_general | solution.py:60
  446.5 12.8 %copy.33 = bf16[2,3072,768]{2,1,0:T(8,128)(2,1)} copy(bf16[2,3072,768]{1,2,0:T(8,128)(2,1)} %subtract_convert_fusion) | data formatting | bytes 18874368
  459.2 3.1 convolution_convert_fusion
  (32 shorter events, 0.4 us)
Async XLA Ops:
  7.2 90.5 %copy-start = (bf16[2,1024,768]{2,1,0:T(8,128)(2,1)S(1)}, bf16[2,1024,768]{2,1,0:T(8,128)(2,1)}, u32[]{:S(2)}) copy-start(bf16[2,1024,768]{2,1,0:T(8,128)(2,1)} %param.4) | copy-start | bytes 9437188
  7.2 192.9 %reduce-scatter.2.cloned.1.call-start = ((), (), s32[]{:S(2)}) async-start(), calls=%async_computation.1 | async-start | bytes 1966080 | tf_op jit(solution)/shard_map/reduce_scatter | solution.py:47
  7.2 37.6 %collective-permute-start = (bf16[2,256,3072]{2,1,0:T(8,128)(2,1)}, bf16[2,256,3072]{2,1,0:T(8,128)(2,1)S(1)}, u32[]{:S(2)}, u32[]{:S(2)}) collective-permute-start(bf16[2,256,3072]{2,1,0:T(8,128)(2,1)} %param.5), channel_id=1, source_target_pairs={{0,3},{1,0},{2,1},{3,2},{4,7},{5,4},{6,5},{7,6},{8,11},{9,8},{10,9... | collective-permute-start | bytes 9437192 | tf_op jit(solution)/shard_map/ppermute | solution.py:36
  44.8 1.7 copy-start.4
  46.5 36.6 %collective-permute-start.1 = (bf16[2,256,3072]{2,1,0:T(8,128)(2,1)S(1)}, bf16[2,256,3072]{2,1,0:T(8,128)(2,1)}, u32[]{:S(2)}, u32[]{:S(2)}) collective-permute-start(bf16[2,256,3072]{2,1,0:T(8,128)(2,1)S(1)} %collective-permute-done), channel_id=1, source_target_pairs={{0,3},{1,0},{2,1},{3,2},{4,7},{5,4},{6,5},{7,6},{8,11},{9,8},{10,9... | collective-permute-start | bytes 9437192 | tf_op jit(solution)/shard_map/ppermute | solution.py:36
  83.1 42.0 %collective-permute-start.2 = (bf16[2,256,3072]{2,1,0:T(8,128)(2,1)}, bf16[2,256,3072]{2,1,0:T(8,128)(2,1)}, u32[]{:S(2)}, u32[]{:S(2)}) collective-permute-start(bf16[2,256,3072]{2,1,0:T(8,128)(2,1)} %collective-permute-done.1), channel_id=1, source_target_pairs={{0,3},{1,0},{2,1},{3,2},{4,7},{5,4},{6,5},{7,6},{8,11},{9,8},{10,9... | collective-permute-start | bytes 9437192 | tf_op jit(solution)/shard_map/ppermute | solution.py:36
  97.7 9.8 %copy-start.5 = (bf16[2,256,3072]{2,1,0:T(8,128)(2,1)S(1)}, bf16[2,256,3072]{2,1,0:T(8,128)(2,1)}, u32[]{:S(2)}) copy-start(bf16[2,256,3072]{2,1,0:T(8,128)(2,1)} %copy-done.4) | copy-start | bytes 9437188
  125.1 30.0 %copy-start.7 = (f32[2,64,768]{2,1,0:T(8,128)S(1)}, f32[2,64,768]{2,1,0:T(8,128)}, u32[]{:S(2)}) copy-start(f32[2,64,768]{2,1,0:T(8,128)} %param.7) | copy-start | bytes 1179652
  171.6 103.7 %all-reduce.3.cloned.1.call-start = ((), (), s32[]{:S(2)}) async-start(), calls=%async_computation.2 | async-start | bytes 786432 | tf_op jit(solution)/shard_map/psum | solution.py:48
  200.1 132.7 %all-gather.2.cloned.1.call-start = ((), (), s32[]{:S(2)}) async-start(), calls=%async_computation.3 | async-start | bytes 1966080 | tf_op jit(solution)/shard_map/all_gather | solution.py:51
  275.3 37.5 %copy-start.3 = (f32[2,64,768]{2,1,0:T(8,128)S(1)}, f32[2,64,768]{2,1,0:T(8,128)}, u32[]{:S(2)}) copy-start(f32[2,64,768]{2,1,0:T(8,128)} %all-reduce.3.cloned.1.call-done) | copy-start | bytes 1179652
  314.1 112.5 %all-reduce.5.cloned.1.call-start = ((), (), s32[]{:S(2)}) async-start(), calls=%async_computation.4 | async-start | bytes 393216 | tf_op jit(solution)/shard_map/psum | solution.py:53
  332.9 93.7 %copy-start.2 = (f32[2,64,3072]{2,1,0:T(8,128)S(1)}, f32[2,64,3072]{2,1,0:T(8,128)}, u32[]{:S(2)}) copy-start(f32[2,64,3072]{2,1,0:T(8,128)} %all-gather.2.cloned.1.call-done) | copy-start | bytes 4718596
  446.5 12.8 %copy-start.6 = (bf16[2,64,768]{2,1,0:T(8,128)(2,1)S(1)}, bf16[2,64,768]{2,1,0:T(8,128)(2,1)}, u32[]{:S(2)}) copy-start(bf16[2,64,768]{2,1,0:T(8,128)(2,1)} %all-reduce.5.cloned.1.call-done) | copy-start | bytes 589828
  446.5 15.8 %copy-start.1 = (bf16[2,1024,768]{2,1,0:T(8,128)(2,1)S(1)}, bf16[2,1024,768]{2,1,0:T(8,128)(2,1)}, u32[]{:S(2)}) copy-start(bf16[2,1024,768]{2,1,0:T(8,128)(2,1)} %param.4) | copy-start | bytes 9437188
Sparse Core Ops, SparseCore 0:
  171.7 28.3 reduce-scatter.1
  203.5 71.7 all-reduce.2
  314.2 18.6 all-gather.1
  355.8 70.6 all-reduce.4
